TPU v7x, 512 devices: a whole 4x8x8 slice. The times are simulated.
512 devices in a mesh: rows: 64 (over y, z), grp: 8 (over x, core).
Axes of the slice: x: 4, y: 8, z: 8, core: 2. Of those that a mesh axis runs over, the one named last changes fastest.
Arguments:
- basis: float32 [64, 2097152], P(None, ('rows', 'grp'))
- values: float32 [64], replicated, may hold values from 0.5 to 20
- archive: bfloat16 [64, 2097152], P('grp', 'rows')
- window_ids: int32 [32], replicated, may hold values from 0 to 63, as said below
Outputs:
- filtered: float32 [96, 2097152], P(None, ('rows', 'grp'))
- projector: float32 [96, 96], replicated
- novelty: float32 [32], replicated
Inputs may be any that keep to these rules, and one draw needn't show every extreme that they name: `window_ids`: distinct; 0 and 63 are always among them.
All inputs are finite; a program needn't handle non-finite values.
Results may differ from a plain program's by a relative error of at most 0.0003.
Values may be sent and summed in bfloat16 or wider, within the bound.
No kernel may reach another device: no remote copies, remote signals or barrier semaphores. Data moves between devices by JAX's collectives and lax.ppermute only.
A program may use at most 64 MiB of HBM per device.

v0:
```python
import math
import jax
import jax.numpy as jnp
from jax import lax
from jax.sharding import PartitionSpec as P

NEWTON = 10
HIGH = lax.Precision.HIGHEST


def spectral(core):
    width = core.shape[0]
    identity = jnp.eye(width, dtype=jnp.float32)
    square = jnp.dot(core, core.T, precision=HIGH)
    total = jnp.trace(square)
    shifted = (square - total / width * identity) / total
    for iteration in range(NEWTON):
        cubed = jnp.dot(jnp.dot(shifted, shifted, precision=HIGH), shifted, precision=HIGH)
        shifted = 1.5 * shifted - 0.5 * cubed
    return 0.5 * (identity + shifted)


def inverse_lower(gram):
    factor = jnp.linalg.cholesky(gram)
    identity = jnp.eye(gram.shape[0], dtype=jnp.float32)
    return (factor, jax.scipy.linalg.solve_triangular(factor, identity, lower=True))


def per_device(basis, values, archive, window_ids):
    mode_count = basis.shape[0]
    window_count = window_ids.shape[0]
    local_rows = basis.shape[1]
    total_rows = local_rows * lax.axis_size("rows") * lax.axis_size("grp")
    everything = lax.all_to_all(archive, "grp", split_axis=1, concat_axis=0, tiled=True)
    picker = (
        window_ids[:, None] == jnp.arange(everything.shape[0], dtype=jnp.int32)[None, :]
    ).astype(jnp.bfloat16)
    gathered = jnp.dot(picker, everything, preferred_element_type=jnp.float32)
    columns = gathered * (1.0 / math.sqrt(total_rows))
    proj_part = jnp.einsum("kr,pr->kp", basis, columns, precision=HIGH)
    energy_part = jnp.sum(columns * columns, axis=1)
    projection, energy = lax.psum((proj_part, energy_part), ("rows", "grp"))
    resid = columns - jnp.einsum("kp,kr->pr", projection, basis, precision=HIGH)
    gram_one = lax.psum(jnp.einsum("pr,qr->pq", resid, resid, precision=HIGH), ("rows", "grp"))
    factor_one, inverse_one = inverse_lower(gram_one)
    first = jnp.dot(inverse_one, resid, precision=HIGH)
    gram_two = lax.psum(jnp.einsum("pr,qr->pq", first, first, precision=HIGH), ("rows", "grp"))
    factor_two, inverse_two = inverse_lower(gram_two)
    ortho = jnp.dot(inverse_two, first, precision=HIGH)
    upper = jnp.dot(factor_two.T, factor_one.T, precision=HIGH)
    top_rows = jnp.concatenate([jnp.diag(values), projection], axis=1)
    low_rows = jnp.concatenate([jnp.zeros((window_count, mode_count), jnp.float32), upper], axis=1)
    core = jnp.concatenate([top_rows, low_rows], axis=0)
    projector = spectral(core)
    weights = jnp.dot(core.T, projector, precision=HIGH)
    stacked = jnp.concatenate([basis, ortho], axis=0)
    filtered = jnp.dot(weights, stacked, precision=HIGH) * math.sqrt(total_rows)
    novelty = jnp.diagonal(gram_one) / energy
    return (filtered, projector, novelty)


def solution(mesh):
    placed = (P(None, ("rows", "grp")), P(), P("grp", "rows"), P())
    return jax.shard_map(
        per_device,
        mesh=mesh,
        in_specs=placed,
        out_specs=(P(None, ("rows", "grp")), P(), P()),
        check_vma=False,
    )
```

profile of v0, /device:TPU:26, one launch (start us, length us, event | category | flops | bytes accessed | tf_op | source)
XLA Modules:
  0.0 340.1 jit_solution(17657873917726056590)
XLA Ops:
  0.6 5.0 %all-to-all-start = ((bf16[8,8,4096]{2,0,1:T(8,128)(2,1)}), bf16[8,8,4096]{2,0,1:T(8,128)(2,1)S(1)}, u32[]{:S(2)}, u32[]{:S(2)}) async-start(bf16[8,8,4096]{2,0,1:T(8,128)(2,1)} %bitcast.81), calls=%async_computation | async-start | bytes 1048576 | tf_op jit(solution)/shard_map/all_to_all | solution.py:34
  5.6 0.7 fusion.16
  6.4 8.1 %all-to-all-done = bf16[8,8,4096]{2,0,1:T(8,128)(2,1)S(1)} async-done(((bf16[8,8,4096]{2,0,1:T(8,128)(2,1)}), bf16[8,8,4096]{2,0,1:T(8,128)(2,1)S(1)}, u32[]{:S(2)}, u32[]{:S(2)}) %all-to-all-start) | async-done | bytes 524320 | tf_op jit(solution)/shard_map/all_to_all | solution.py:34
  14.5 1.0 multiply_reduce_fusion
  15.5 1.0 convolution_bitcast_fusion
  16.5 104.3 %psum.28 = f32[64,32]{0,1:T(8,128)S(1)} all-reduce(f32[64,32]{0,1:T(8,128)S(1)} %convolution_bitcast_fusion), channel_id=1, replica_groups=mesh['rows'=64,'grp'=8] {'rows','grp'}, use_global_device_ids=true, to_apply=%region_0.0 | all-reduce | flops 2048 | bytes 16384 | tf_op jit(solution)/shard_map/psum | solution.py:42
  120.8 0.6 convolution_subtract_fusion
  121.5 0.6 fusion.51
  122.0 94.5 %psum.29 = f32[32,32]{0,1:T(8,128)S(1)} all-reduce(f32[32,32]{0,1:T(8,128)S(1)} %fusion.51), channel_id=1, replica_groups=mesh['rows'=64,'grp'=8] {'rows','grp'}, use_global_device_ids=true, to_apply=%region_1.0 | all-reduce | flops 1024 | bytes 8192 | tf_op jit(solution)/shard_map/psum | solution.py:44
  216.6 2.9 cholesky.44
  219.6 0.6 compare_reduce_fusion.1
  220.2 0.7 fusion.29
  220.9 2.4 custom-call.8
  223.3 0.2 fusion.19
  223.6 0.6 fusion.52
  224.1 0.6 fusion.53
  224.7 95.4 %all-reduce.1 = (f32[32,32]{0,1:T(8,128)S(1)}, f32[32]{0:T(128)S(1)}) all-reduce(f32[32,32]{0,1:T(8,128)S(1)} %fusion.53, f32[32]{0:T(128)S(1)} %get-tuple-element.7), channel_id=1, replica_groups=mesh['rows'=64,'grp'=8] {'rows','grp'}, use_global_device_ids=true, to_apply=%region_4.0 | all-reduce | flops 1056 | bytes 8448 | tf_op jit(solution)/shard_map/psum | solution.py:47
  320.2 2.9 cholesky.55
  323.2 0.6 compare_reduce_fusion
  323.8 1.5 fusion.30
  325.3 0.7 select_bitcast_fusion
  326.0 0.7 gather_fusion
  326.7 2.4 custom-call.9
  329.1 0.2 fusion.17
  329.4 0.6 fusion.63
  330.0 0.9 select_reduce_fusion
  331.5 0.8 fusion.34
  332.4 0.8 fusion.14
  336.4 0.2 fusion.5
  336.6 0.3 fusion.32
  337.0 0.5 div.21
  337.5 2.6 convolution_multiply_fusion
  (29 shorter events, 3.4 us)
Async XLA Ops:
  0.6 14.9 %copy-start = (f32[64,4096]{1,0:T(8,128)S(1)}, f32[64,4096]{1,0:T(8,128)}, u32[]{:S(2)}) copy-start(f32[64,4096]{1,0:T(8,128)} %param.7) | copy-start | bytes 3145732
  0.6 13.8 %all-to-all-start = ((bf16[8,8,4096]{2,0,1:T(8,128)(2,1)}), bf16[8,8,4096]{2,0,1:T(8,128)(2,1)S(1)}, u32[]{:S(2)}, u32[]{:S(2)}) async-start(bf16[8,8,4096]{2,0,1:T(8,128)(2,1)} %bitcast.81), calls=%async_computation | async-start | bytes 1048576 | tf_op jit(solution)/shard_map/all_to_all | solution.py:34
  336.6 3.5 %copy-start.1 = (f32[96,96]{1,0:T(8,128)}, f32[96,96]{1,0:T(8,128)S(1)}, u32[]{:S(2)}) copy-start(f32[96,96]{1,0:T(8,128)S(1)} %fusion.5) | copy-start | bytes 110596
where the time goes:
time: 341 us; the launch traced here: 340 us
  blocking collectives  294 us (86%)
  matrix products  15.7 us (5%)
  other arithmetic  14.7 us (4%)
  waiting for transfers between devices  8.12 us (2%)
  starting transfers between devices  4.97 us (1%)
    psum x1, blocking collectives, per_device(): projection, energy = lax.psum((proj_part, energy_part), ('rows', 'grp'))  104 us
    psum x1, blocking collectives, per_device(): lax.psum(jnp.einsum('pr,qr->pq', first, first, precision=HIGH), ('rows',...  95.4 us
    psum x1, blocking collectives, per_device(): lax.psum(jnp.einsum('pr,qr->pq', resid, resid, precision=HIGH), ('rows',...  94.5 us
    all_to_all x1, waiting for transfers between devices, per_device(): lax.all_to_all(archive, 'grp', split_axis=1, concat_axis=0, tiled=True)  8.12 us
    another operation x6, other arithmetic, inverse_lower(): factor = jnp.linalg.cholesky(gram)  7.19 us
  transfers between devices with their start and end apart: 1, of which 1 were waited for; matrix products, arithmetic and copies ran while one was open for 0% of the time, Pallas kernels for 0%

commit v1 on v0

--- a/solution.py
+++ b/solution.py
@@ -6,6 +6,11 @@
 
 NEWTON = 10
 HIGH = lax.Precision.HIGHEST
+
+
+def by_each_axis(value, leading, second):
+    inner = lax.psum(value, leading)
+    return lax.psum(inner, second)
 
 
 def spectral(core):
@@ -39,7 +44,7 @@
     columns = gathered * (1.0 / math.sqrt(total_rows))
     proj_part = jnp.einsum("kr,pr->kp", basis, columns, precision=HIGH)
     energy_part = jnp.sum(columns * columns, axis=1)
-    projection, energy = lax.psum((proj_part, energy_part), ("rows", "grp"))
+    projection, energy = by_each_axis((proj_part, energy_part), "rows", "grp")
     resid = columns - jnp.einsum("kp,kr->pr", projection, basis, precision=HIGH)
     gram_one = lax.psum(jnp.einsum("pr,qr->pq", resid, resid, precision=HIGH), ("rows", "grp"))
     factor_one, inverse_one = inverse_lower(gram_one)

time: 341 us -> 545 us (1.60)
  the two profiles are of different devices: /device:TPU:26 before, /device:TPU:1 now
where the time goes in v1:
time: 545 us
  blocking collectives  493 us (90%)
  matrix products  15.7 us (3%)
  other arithmetic  14.7 us (3%)
  starting transfers between devices  10.4 us (2%)
  waiting for transfers between devices  8.64 us (2%)
    psum x1, blocking collectives, by_each_axis(): inner = lax.psum(value, leading)  227 us
    psum x1, blocking collectives, per_device(): lax.psum(jnp.einsum('pr,qr->pq', first, first, precision=HIGH), ('rows',...  95.5 us
    psum x1, blocking collectives, per_device(): lax.psum(jnp.einsum('pr,qr->pq', resid, resid, precision=HIGH), ('rows',...  95.1 us
    psum x1, blocking collectives, by_each_axis(): return lax.psum(inner, second)  75.8 us
  transfers between devices with their start and end apart: 1, of which 1 were waited for; matrix products, arithmetic and copies ran while one was open for 0% of the time, Pallas kernels for 0%

profile of v1, /device:TPU:1, one launch (start us, length us, event | category | flops | bytes accessed | tf_op | source)
XLA Modules:
  0.0 544.8 jit_solution(2936949378837340428)
XLA Ops:
  0.6 10.4 %all-to-all-start = ((bf16[8,8,4096]{2,0,1:T(8,128)(2,1)}), bf16[8,8,4096]{2,0,1:T(8,128)(2,1)S(1)}, u32[]{:S(2)}, u32[]{:S(2)}) async-start(bf16[8,8,4096]{2,0,1:T(8,128)(2,1)} %bitcast.81), calls=%async_computation | async-start | bytes 1048576 | tf_op jit(solution)/shard_map/all_to_all | solution.py:39
  11.0 0.7 fusion.16
  11.8 8.6 %all-to-all-done = bf16[8,8,4096]{2,0,1:T(8,128)(2,1)S(1)} async-done(((bf16[8,8,4096]{2,0,1:T(8,128)(2,1)}), bf16[8,8,4096]{2,0,1:T(8,128)(2,1)S(1)}, u32[]{:S(2)}, u32[]{:S(2)}) %all-to-all-start) | async-done | bytes 524320 | tf_op jit(solution)/shard_map/all_to_all | solution.py:39
  20.4 1.0 multiply_reduce_fusion
  21.4 1.0 convolution_bitcast_fusion
  22.4 226.6 %all-reduce.1 = (f32[64,32]{0,1:T(8,128)S(1)}, f32[32]{0:T(128)S(1)}) all-reduce(f32[64,32]{0,1:T(8,128)S(1)} %convolution_bitcast_fusion, f32[32]{0:T(128)S(1)} %get-tuple-element.9), channel_id=1, replica_groups=mesh['rows'=64,'grp'=8] {'rows'}, use_global_device_ids=true, to_apply=%region_0.0 | all-reduce | flops 2080 | bytes 16640 | tf_op jit(solution)/shard_map/psum | solution.py:12
  249.0 75.8 %all-reduce.2 = (f32[64,32]{0,1:T(8,128)S(1)}, f32[32]{0:T(128)S(1)}) all-reduce(f32[64,32]{0,1:T(8,128)S(1)} %get-tuple-element.5, f32[32]{0:T(128)S(1)} %get-tuple-element.6), channel_id=1, replica_groups=mesh['rows'=64,'grp'=8] {'grp'}, use_global_device_ids=true, to_apply=%region_1.0 | all-reduce | flops 2080 | bytes 16640 | tf_op jit(solution)/shard_map/psum | solution.py:13
  324.8 0.6 convolution_subtract_fusion
  325.5 0.6 fusion.51
  326.1 95.1 %psum.44 = f32[32,32]{0,1:T(8,128)S(1)} all-reduce(f32[32,32]{0,1:T(8,128)S(1)} %fusion.51), channel_id=1, replica_groups=mesh['rows'=64,'grp'=8] {'rows','grp'}, use_global_device_ids=true, to_apply=%region_2.0 | all-reduce | flops 1024 | bytes 8192 | tf_op jit(solution)/shard_map/psum | solution.py:49
  421.3 2.9 cholesky.44
  424.3 0.6 compare_reduce_fusion.1
  424.9 0.7 fusion.29
  425.6 2.4 custom-call.8
  428.0 0.2 fusion.19
  428.2 0.6 fusion.52
  428.8 0.6 fusion.53
  429.4 95.5 %psum.45 = f32[32,32]{0,1:T(8,128)S(1)} all-reduce(f32[32,32]{0,1:T(8,128)S(1)} %fusion.53), channel_id=1, replica_groups=mesh['rows'=64,'grp'=8] {'rows','grp'}, use_global_device_ids=true, to_apply=%region_5.8 | all-reduce | flops 1024 | bytes 8192 | tf_op jit(solution)/shard_map/psum | solution.py:52
  525.0 2.9 cholesky.55
  527.9 0.6 compare_reduce_fusion
  528.6 1.5 fusion.30
  530.1 0.7 select_bitcast_fusion
  530.7 0.7 gather_fusion
  531.5 2.4 custom-call.9
  533.9 0.2 fusion.17
  534.1 0.6 fusion.63
  534.7 0.9 select_reduce_fusion
  536.3 0.8 fusion.34
  537.1 0.8 fusion.14
  541.4 0.3 fusion.32
  541.7 0.5 div.21
  542.2 2.6 convolution_multiply_fusion
  (30 shorter events, 3.6 us)
Async XLA Ops:
  0.6 20.8 %copy-start = (f32[64,4096]{1,0:T(8,128)S(1)}, f32[64,4096]{1,0:T(8,128)}, u32[]{:S(2)}) copy-start(f32[64,4096]{1,0:T(8,128)} %param.7) | copy-start | bytes 3145732
  0.6 19.8 %all-to-all-start = ((bf16[8,8,4096]{2,0,1:T(8,128)(2,1)}), bf16[8,8,4096]{2,0,1:T(8,128)(2,1)S(1)}, u32[]{:S(2)}, u32[]{:S(2)}) async-start(bf16[8,8,4096]{2,0,1:T(8,128)(2,1)} %bitcast.81), calls=%async_computation | async-start | bytes 1048576 | tf_op jit(solution)/shard_map/all_to_all | solution.py:39
  541.3 3.5 copy-start.1
